TPU v7x, 256 devices: a whole 4x4x8 slice. The times are simulated.
256 devices in a mesh: row: 2 (over core), col: 128 (over z, y, x).
Axes of the slice: x: 4, y: 4, z: 8, core: 2. Of those that a mesh axis runs over, the one named last changes fastest.
Arguments:
- image_tokens: bfloat16 [64, 4096, 256], P('row', 'col'), may hold values from -6 to 6
- w_in: bfloat16 [256, 768], replicated, may hold values from -0.375 to 0.375
- conv_kernel: bfloat16 [3, 3, 768], replicated, may hold values from -2 to 2
- conv_bias: float32 [768], replicated, may hold values from -3 to 3
- long_filter: bfloat16 [64, 256], replicated, may hold values from -0.75 to 0.75
- skip_gain: float32 [256], replicated, may hold values from 0.5 to 1.5
- w_out: bfloat16 [256, 256], replicated, may hold values from -0.375 to 0.375
Outputs:
- layer_out: bfloat16 [64, 4096, 256], P('row', 'col')
All inputs are finite; a program needn't handle non-finite values.
Results may differ from a plain program's by a relative error of at most 0.014.
Values may be sent and summed in bfloat16 or wider, within the bound.
A program may use at most 64 MiB of HBM per device.

v0:
```python
import jax
import jax.numpy as jnp
from jax import lax
from jax.sharding import PartitionSpec as P


def extended(block, sides, width):
    for axis, dim in sides:
        count = lax.axis_size(axis)
        forward = [(i, i + 1) for i in range(count - 1)]
        backward = [(target, source) for source, target in forward]
        low = lax.ppermute(
            lax.slice_in_dim(block, block.shape[dim] - width, None, axis=dim), axis, forward
        )
        high = lax.ppermute(lax.slice_in_dim(block, 0, width, axis=dim), axis, backward)
        block = jnp.concatenate([low, block, high], axis=dim)
    return block


def depthwise(padded, kernel, bias, height, span):
    total = jnp.zeros((height, span, padded.shape[2]), jnp.float32) + bias
    for row_off in range(3):
        for col_off in range(3):
            window = padded[row_off : row_off + height, col_off : col_off + span, :].astype(
                jnp.float32
            )
            total = total + window * kernel[row_off, col_off].astype(jnp.float32)
    return total.astype(jnp.bfloat16)


def toeplitz(filt_rev, offset, out_count, src_count):
    margin = filt_rev.shape[0] // 3
    spare = margin // 2
    length = out_count + src_count - 1
    start = jnp.asarray(margin + margin - 1 - spare - (out_count - 1), jnp.int32) - jnp.asarray(
        offset, jnp.int32
    )
    window = lax.dynamic_slice_in_dim(filt_rev, start, length, 0)
    tiled = jnp.tile(window, (out_count + 1, 1))
    strided = tiled[out_count - 1 : out_count - 1 + out_count * (length - 1)]
    return strided.reshape(out_count, length - 1, filt_rev.shape[1])[:, :src_count]


def on_device(image_tokens, w_in, conv_kernel, conv_bias, long_filter, skip_gain, w_out):
    row_count, col_count, width = image_tokens.shape
    flat = image_tokens.reshape(row_count * col_count, width)
    projected = jnp.dot(flat, w_in, preferred_element_type=jnp.float32)
    projected = projected.astype(jnp.bfloat16).reshape(row_count, col_count, 3 * width)
    padded = extended(projected, (("row", 0), ("col", 1)), 1)
    mixed = depthwise(padded, conv_kernel, conv_bias, row_count, col_count)
    query = mixed[:, :, :width].astype(jnp.float32)
    key = mixed[:, :, width : 2 * width].astype(jnp.float32)
    value = mixed[:, :, 2 * width :].astype(jnp.float32)
    product = (key * value).astype(jnp.bfloat16)
    filt_pad = jnp.concatenate([jnp.zeros_like(long_filter), long_filter], axis=0)
    zero_band = jnp.zeros_like(filt_pad)
    filt_rev = jnp.concatenate([zero_band, jnp.flip(filt_pad, 0), zero_band], axis=0)
    my_start = lax.axis_index("row") * row_count
    empty_long = jnp.zeros((row_count, col_count, width), jnp.float32)
    total = empty_long
    piece = lax.all_gather(product, "row", axis=0, tiled=True)
    start = jnp.int32(0)
    piece_len = piece.shape[0]
    step_len = min(row_count, piece_len)
    for offset_row in range(0, piece_len, step_len):
        sub_piece = piece[offset_row : offset_row + step_len]
        sub_start = start + offset_row

        def work(running):
            toeplitz_block = toeplitz(filt_rev, my_start - sub_start, row_count, step_len)
            return running + jnp.einsum(
                "abc,bwc->awc", toeplitz_block, sub_piece, preferred_element_type=jnp.float32
            )

        def keep(running):
            return running

        total = lax.cond(sub_start < my_start + row_count, work, keep, total)
    gated = (query * (total + skip_gain * product.astype(jnp.float32))).astype(jnp.bfloat16)
    gated_flat = gated.reshape(row_count * col_count, width)
    final = jnp.dot(gated_flat, w_out, preferred_element_type=jnp.float32)
    return final.astype(jnp.bfloat16).reshape(row_count, col_count, width)


def solution(mesh):
    in_specs = (P("row", "col", None), P(), P(), P(), P(), P(), P())
    out_specs = P("row", "col", None)
    return jax.shard_map(
        on_device, mesh=mesh, in_specs=in_specs, out_specs=out_specs, check_vma=False
    )
```

profile of v0, /device:TPU:1, one launch (start us, length us, event | category | flops | bytes accessed | tf_op | source)
XLA Modules:
  0.0 115.1 jit_solution(9710104501801222011)
XLA Ops:
  6.5 1.0 copy-done
  7.6 1.6 %convolution_convert_fusion = bf16[1024,768]{1,0:T(8,128)(2,1)S(1)} fusion(bf16[1024,256]{1,0:T(8,128)(2,1)S(1)} %bitcast.18, bf16[256,768]{1,0:T(8,128)(2,1)} %param.12), kind=kOutput, calls=%fused_computation.9 | convolution fusion | flops 403439616 | bytes 2490368 | tf_op jit(solution)/shard_map/dot_general | solution.py:47
  9.2 1.3 %collective-permute-start = (bf16[1,32,768]{2,1,0:T(8,128)(2,1)S(1)}, bf16[1,32,768]{2,1,0:T(8,128)(2,1)S(1)}, u32[]{:S(2)}, u32[]{:S(2)}) collective-permute-start(bf16[1,32,768]{2,1,0:T(8,128)(2,1)S(1)} %get-tuple-element.63), channel_id=1, source_target_pairs={{0,128},{1,129},{2,130},{3,131},{4,132},{5,133},{6,134},{7,135},{8... | collective-permute-start | bytes 147464 | tf_op jit(solution)/shard_map/ppermute | solution.py:12
  10.5 5.1 %collective-permute-start.1 = (bf16[1,32,768]{2,1,0:T(8,128)(2,1)S(1)}, bf16[1,32,768]{2,1,0:T(8,128)(2,1)S(1)}, u32[]{:S(2)}, u32[]{:S(2)}) collective-permute-start(bf16[1,32,768]{2,1,0:T(8,128)(2,1)S(1)} %get-tuple-element.64), channel_id=1, source_target_pairs={{128,0},{129,1},{130,2},{131,3},{132,4},{133,5},{134,6},{135,7},{1... | collective-permute-start | bytes 147464 | tf_op jit(solution)/shard_map/ppermute | solution.py:15
  15.6 0.9 collective-permute-done.1
  16.7 1.8 %collective-permute-start.2 = (bf16[34,1,768]{2,1,0:T(2,128)(2,1)S(1)}, bf16[34,1,768]{2,1,0:T(2,128)(2,1)S(1)}, u32[]{:S(2)}, u32[]{:S(2)}) collective-permute-start(bf16[34,1,768]{2,1,0:T(2,128)(2,1)S(1)} %get-tuple-element.61), channel_id=1, source_target_pairs={{0,1},{1,2},{2,3},{3,4},{4,5},{5,6},{6,7},{7,8},{8,9},{9,10},{10,1... | collective-permute-start | bytes 156680 | tf_op jit(solution)/shard_map/ppermute | solution.py:12
  18.5 1.3 %collective-permute-start.3 = (bf16[34,1,768]{2,1,0:T(2,128)(2,1)S(1)}, bf16[34,1,768]{2,1,0:T(2,128)(2,1)S(1)}, u32[]{:S(2)}, u32[]{:S(2)}) collective-permute-start(bf16[34,1,768]{2,1,0:T(2,128)(2,1)S(1)} %get-tuple-element.62), channel_id=1, source_target_pairs={{1,0},{2,1},{3,2},{4,3},{5,4},{6,5},{7,6},{8,7},{9,8},{10,9},{11,1... | collective-permute-start | bytes 156680 | tf_op jit(solution)/shard_map/ppermute | solution.py:15
  19.9 0.5 collective-permute-done.2
  20.4 3.8 %collective-permute-done.3 = bf16[34,1,768]{2,1,0:T(2,128)(2,1)S(1)} collective-permute-done((bf16[34,1,768]{2,1,0:T(2,128)(2,1)S(1)}, bf16[34,1,768]{2,1,0:T(2,128)(2,1)S(1)}, u32[]{:S(2)}, u32[]{:S(2)}) %collective-permute-start.3) | collective-permute-done | bytes 52256 | tf_op jit(solution)/shard_map/ppermute | solution.py:15
  24.2 1.2 %maximum_maximum_fusion = (bf16[34,33,768]{2,1,0:T(8,128)(2,1)S(1)}, bf16[34,33,768]{2,1,0:T(8,128)(2,1)S(1)}) fusion(bf16[1,32,768]{2,1,0:T(8,128)(2,1)S(1)} %collective-permute-done.1, bf16[32,32,768]{2,1,0:T(8,128)(2,1)S(1)} %bitcast.20, bf16[1,32,768]{2,1,0:T(8,128)(2,1)S(1)} %collective-permute-done, bf16[34,1,768]{2,1,0:T(2,128)(2,1)S(1)} %collective-permute-done.2, ...), kind=kLoop, calls=%fused_computation.7 | loop fusion | flops 13787136 | bytes 5222400 | tf_op jit(solution)/shard_map/concatenate | solution.py:16
  25.5 4.1 %add_convert_fusion = bf16[32,32,768]{2,1,0:T(8,128)(2,1)S(1)} fusion(bf16[32,32,768]{2,1,0:T(8,128)(2,1)S(1)} %bitcast.21, bf16[34,33,768]{2,1,0:T(8,128)(2,1)S(1)} %get-tuple-element.60, bf16[1,32,768]{2,1,0:T(8,128)(2,1)S(1)} %collective-permute-done.1, bf16[34,33,768]{2,1,0:T(8,128)(2,1)S(1)} %get-tuple-element.59, ...), kind=kLoop, calls=%fused_computation.6 | loop fusion | flops 23592960 | bytes 12711936 | tf_op jit(solution)/shard_map/convert_element_type | solution.py:28
  29.6 0.9 multiply_convert_fusion.1
  30.7 22.5 %all-gather.2.cloned.1.call-done = bf16[64,32,256]{2,1,0:T(8,128)(2,1)} async-done(((bf16[32,32,256]{2,1,0:T(8,128)(2,1)}), bf16[64,32,256]{2,1,0:T(8,128)(2,1)}) %all-gather.2.cloned.1.call-update) | async-done | bytes 1048592 | tf_op jit(solution)/shard_map/all_gather | solution.py:61
  53.2 24.2 %conditional.2 = (f32[32,32,256]{1,0,2:T(8,128)}) conditional(s32[]{:T(128)} %convert_element_type.91, () %tuple.17, (s32[]{:T(128)}, bf16[384,256]{1,0:T(8,128)(2,1)S(1)}, bf16[64,32,256]{2,1,0:T(8,128)(2,1)}) %tuple.18), branch_computations={%region_0.1_spmd, %region_1.2_spmd} | conditional | flops 16777220 | bytes 20984918 | solution.py:78
  53.4 1.3 %tile.10 = bf16[2079,256]{1,0:T(8,128)(2,1)} reshape(bf16[33,63,256]{2,1,0:T(8,128)(2,1)S(1)} %tile.4) | data formatting | bytes 2128896 | tf_op jit(solution)/shard_map/cond/branch_1_fun/tile | solution.py:39
  54.7 2.5 %slice.133 = bf16[1984,256]{1,0:T(8,128)(2,1)} slice(bf16[2079,256]{1,0:T(8,128)(2,1)} %tile.10), slice={[31:2015], [0:256]} | slice | bytes 2031616 | tf_op jit(solution)/shard_map/cond/branch_1_fun/slice | solution.py:40
  57.2 2.3 %reshape.24 = bf16[32,62,256]{2,1,0:T(8,128)(2,1)} reshape(bf16[1984,256]{1,0:T(8,128)(2,1)} %slice.133) | data formatting | bytes 2031616 | tf_op jit(solution)/shard_map/cond/branch_1_fun/reshape | solution.py:41
  59.5 1.9 %slice.134 = bf16[32,32,256]{2,1,0:T(8,128)(2,1)} slice(bf16[32,62,256]{2,1,0:T(8,128)(2,1)} %reshape.24), slice={[0:32], [0:32], [0:256]} | slice | bytes 1048576 | tf_op jit(solution)/shard_map/cond/branch_1_fun/slice | solution.py:41
  61.4 4.6 %copy.29 = bf16[32,32,256]{1,0,2:T(8,128)(2,1)} copy(bf16[32,32,256]{2,1,0:T(8,128)(2,1)} %slice.134) | data formatting | bytes 1048576 | tf_op jit(solution)/shard_map/cond
  66.0 6.5 %copy.24 = bf16[64,32,256]{1,0,2:T(8,128)(2,1)} copy(bf16[64,32,256]{2,1,0:T(8,128)(2,1)S(1)} %copy-done.1) | data formatting | bytes 2097152 | tf_op jit(solution)/shard_map
  72.5 4.9 %convolution_bitcast_fusion = f32[32,32,256]{1,0,2:T(8,128)} fusion(bf16[32,32,256]{1,0,2:T(8,128)(2,1)} %copy.29, bf16[64,32,256]{1,0,2:T(8,128)(2,1)} %copy.24), kind=kOutput, calls=%fused_computation | convolution fusion | flops 16777216 | bytes 5242880 | tf_op jit(solution)/shard_map/cond/branch_1_fun/abc,bwc->awc/dot_general | solution.py:71
  77.4 28.8 %conditional.3 = (f32[32,32,256]{2,1,0:T(8,128)S(1)}) conditional(s32[]{:T(128)} %convert_element_type.90, f32[32,32,256]{1,0,2:T(8,128)} %get-tuple-element.67, (s32[]{:T(128)}, bf16[384,256]{1,0:T(8,128)(2,1)S(1)}, bf16[64,32,256]{2,1,0:T(8,128)(2,1)}, f32[32,32,256]{1,0,2:T(8,128)}) %tuple.19), branch_computations={%region_2.3_spmd, %region_3.4_spmd} | conditional | flops 17039364 | bytes 27276386 | solution.py:78
  77.6 1.3 %tile.12 = bf16[2079,256]{1,0:T(8,128)(2,1)} reshape(bf16[33,63,256]{2,1,0:T(8,128)(2,1)S(1)} %tile.11) | data formatting | bytes 2128896 | tf_op jit(solution)/shard_map/cond/branch_1_fun/tile | solution.py:39
  78.9 2.4 %slice.136 = bf16[1984,256]{1,0:T(8,128)(2,1)} slice(bf16[2079,256]{1,0:T(8,128)(2,1)} %tile.12), slice={[31:2015], [0:256]} | slice | bytes 2031616 | tf_op jit(solution)/shard_map/cond/branch_1_fun/slice | solution.py:40
  81.3 2.4 %reshape.25 = bf16[32,62,256]{2,1,0:T(8,128)(2,1)} reshape(bf16[1984,256]{1,0:T(8,128)(2,1)} %slice.136) | data formatting | bytes 2031616 | tf_op jit(solution)/shard_map/cond/branch_1_fun/reshape | solution.py:41
  83.7 1.9 %slice.137 = bf16[32,32,256]{2,1,0:T(8,128)(2,1)} slice(bf16[32,62,256]{2,1,0:T(8,128)(2,1)} %reshape.25), slice={[0:32], [0:32], [0:256]} | slice | bytes 1048576 | tf_op jit(solution)/shard_map/cond/branch_1_fun/slice | solution.py:41
  85.5 4.6 %copy.30 = bf16[32,32,256]{1,0,2:T(8,128)(2,1)} copy(bf16[32,32,256]{2,1,0:T(8,128)(2,1)} %slice.137) | data formatting | bytes 1048576 | tf_op jit(solution)/shard_map/cond
  90.1 6.5 %copy.25 = bf16[64,32,256]{1,0,2:T(8,128)(2,1)} copy(bf16[64,32,256]{2,1,0:T(8,128)(2,1)S(1)} %copy-done.2) | data formatting | bytes 2097152 | tf_op jit(solution)/shard_map
  96.6 6.1 %bitcast_add_fusion = f32[32,32,256]{1,0,2:T(8,128)} fusion(f32[32,32,256]{1,0,2:T(8,128)} %get-tuple-element.30, bf16[32,32,256]{1,0,2:T(8,128)(2,1)} %copy.30, bf16[64,32,256]{1,0,2:T(8,128)(2,1)} %copy.25), kind=kOutput, calls=%fused_computation.3 | convolution fusion | flops 17039360 | bytes 9437184 | tf_op jit(solution)/shard_map/cond/branch_1_fun/abc,bwc->awc/dot_general | solution.py:71
  102.7 3.5 %copy.28 = f32[32,32,256]{2,1,0:T(8,128)S(1)} copy(f32[32,32,256]{1,0,2:T(8,128)} %bitcast_add_fusion) | data formatting | bytes 2097152 | tf_op jit(solution)/shard_map/cond | solution.py:78
  106.5 0.6 copy-done.3
  107.1 1.1 convolution_convert_fusion.1
  (29 shorter events, 1.0 us)
Async XLA Ops:
  6.5 1.0 copy-start
  6.5 13.3 %copy-start.4 = (bf16[3,3,768]{2,1,0:T(4,128)(2,1)S(1)}, bf16[3,3,768]{2,1,0:T(4,128)(2,1)}, u32[]{:S(2)}) copy-start(bf16[3,3,768]{2,1,0:T(4,128)(2,1)} %param.13) | copy-start | bytes 41476
  6.5 46.7 %all-gather.2.cloned.1.call-start = ((), (), s32[]{:S(2)}) async-start(), calls=%async_computation | async-start | bytes 1572864 | tf_op jit(solution)/shard_map/all_gather | solution.py:61
  9.2 6.5 %collective-permute-start = (bf16[1,32,768]{2,1,0:T(8,128)(2,1)S(1)}, bf16[1,32,768]{2,1,0:T(8,128)(2,1)S(1)}, u32[]{:S(2)}, u32[]{:S(2)}) collective-permute-start(bf16[1,32,768]{2,1,0:T(8,128)(2,1)S(1)} %get-tuple-element.63), channel_id=1, source_target_pairs={{0,128},{1,129},{2,130},{3,131},{4,132},{5,133},{6,134},{7,135},{8... | collective-permute-start | bytes 147464 | tf_op jit(solution)/shard_map/ppermute | solution.py:12
  10.5 6.0 %collective-permute-start.1 = (bf16[1,32,768]{2,1,0:T(8,128)(2,1)S(1)}, bf16[1,32,768]{2,1,0:T(8,128)(2,1)S(1)}, u32[]{:S(2)}, u32[]{:S(2)}) collective-permute-start(bf16[1,32,768]{2,1,0:T(8,128)(2,1)S(1)} %get-tuple-element.64), channel_id=1, source_target_pairs={{128,0},{129,1},{130,2},{131,3},{132,4},{133,5},{134,6},{135,7},{1... | collective-permute-start | bytes 147464 | tf_op jit(solution)/shard_map/ppermute | solution.py:15
  16.6 8.8 %copy-start.6 = (f32[768]{0:T(1024)S(1)}, f32[768]{0:T(1024)}, u32[]{:S(2)}) copy-start(f32[768]{0:T(1024)} %param.14) | copy-start | bytes 9220
  16.7 3.8 %collective-permute-start.2 = (bf16[34,1,768]{2,1,0:T(2,128)(2,1)S(1)}, bf16[34,1,768]{2,1,0:T(2,128)(2,1)S(1)}, u32[]{:S(2)}, u32[]{:S(2)}) collective-permute-start(bf16[34,1,768]{2,1,0:T(2,128)(2,1)S(1)} %get-tuple-element.61), channel_id=1, source_target_pairs={{0,1},{1,2},{2,3},{3,4},{4,5},{5,6},{6,7},{7,8},{8,9},{9,10},{10,1... | collective-permute-start | bytes 156680 | tf_op jit(solution)/shard_map/ppermute | solution.py:12
  18.5 5.7 %collective-permute-start.3 = (bf16[34,1,768]{2,1,0:T(2,128)(2,1)S(1)}, bf16[34,1,768]{2,1,0:T(2,128)(2,1)S(1)}, u32[]{:S(2)}, u32[]{:S(2)}) collective-permute-start(bf16[34,1,768]{2,1,0:T(2,128)(2,1)S(1)} %get-tuple-element.62), channel_id=1, source_target_pairs={{1,0},{2,1},{3,2},{4,3},{5,4},{6,5},{7,6},{8,7},{9,8},{10,9},{11,1... | collective-permute-start | bytes 156680 | tf_op jit(solution)/shard_map/ppermute | solution.py:15
  25.5 5.1 %copy-start.5 = (bf16[64,256]{1,0:T(8,128)(2,1)S(1)}, bf16[64,256]{1,0:T(8,128)(2,1)}, u32[]{:S(2)}) copy-start(bf16[64,256]{1,0:T(8,128)(2,1)} %param.15) | copy-start | bytes 98308
  57.2 8.8 %copy-start.1 = (bf16[64,32,256]{2,1,0:T(8,128)(2,1)S(1)}, bf16[64,32,256]{2,1,0:T(8,128)(2,1)}, u32[]{:S(2)}) copy-start(bf16[64,32,256]{2,1,0:T(8,128)(2,1)} %get-tuple-element.44) | copy-start | bytes 3145732 | tf_op jit(solution)/shard_map/cond
  77.4 28.8 %copy-start.7 = (f32[256]{0:T(256)S(1)}, f32[256]{0:T(256)}, u32[]{:S(2)}) copy-start(f32[256]{0:T(256)} %param.16) | copy-start | bytes 3076
  81.3 8.8 %copy-start.2 = (bf16[64,32,256]{2,1,0:T(8,128)(2,1)S(1)}, bf16[64,32,256]{2,1,0:T(8,128)(2,1)}, u32[]{:S(2)}) copy-start(bf16[64,32,256]{2,1,0:T(8,128)(2,1)} %get-tuple-element.47) | copy-start | bytes 3145732 | tf_op jit(solution)/shard_map/cond
  106.2 0.9 copy-start.3
Sparse Core Ops, SparseCore 0:
  30.7 22.5 all-gather.1
where the time goes:
time: 116 us; the launch traced here: 115 us
  local copies, waits for them, and re-layouts  43.7 us (38%)
  waiting for transfers between devices  27.7 us (24%)
  matrix products  13.7 us (12%)
  between operations  13.6 us (12%)
  starting transfers between devices  9.57 us (8%)
  other arithmetic  6.79 us (6%)
    all_gather x1, waiting for transfers between devices, on_device(): piece = lax.all_gather(product, 'row', axis=0, tiled=True)  22.5 us
    another operation x2, local copies, waits for them, and re-layouts  13 us
    dot_general x2, matrix products, work(): jnp.einsum('abc,bwc->awc', toeplitz_block, sub_piece, preferred_element_t...  11.1 us
    cond x6, local copies, waits for them, and re-layouts  9.15 us
    ppermute x2, starting transfers between devices, extended(): lax.ppermute(lax.slice_in_dim(block, 0, width, axis=dim), axis, backward)  6.44 us
    slice x2, local copies, waits for them, and re-layouts, toeplitz(): strided = tiled[out_count - 1:out_count - 1 + out_count * (length - 1)]  4.91 us
    reshape x2, local copies, waits for them, and re-layouts, toeplitz(): strided.reshape(out_count, length - 1, filt_rev.shape[1])[:, :src_count]  4.73 us
    ppermute x2, waiting for transfers between devices, extended(): lax.ppermute(lax.slice_in_dim(block, 0, width, axis=dim), axis, backward)  4.65 us
  transfers between devices with their start and end apart: 5, of which 4 were waited for; matrix products, arithmetic and copies ran while one was open for 0% of the time, Pallas kernels for 0%

commit v1 on v0

--- a/solution.py
+++ b/solution.py
@@ -58,7 +58,9 @@
     my_start = lax.axis_index("row") * row_count
     empty_long = jnp.zeros((row_count, col_count, width), jnp.float32)
     total = empty_long
-    piece = lax.all_gather(product, "row", axis=0, tiled=True)
+    piece = jnp.concatenate(
+        lax.all_to_all(jnp.stack([product] * lax.axis_size("row")), "row", 0, 0), axis=0
+    )
     start = jnp.int32(0)
     piece_len = piece.shape[0]
     step_len = min(row_count, piece_len)

time: 116 us -> 89.8 us (0.77)
  the two profiles are of different devices: /device:TPU:1 before, /device:TPU:127 now
where the time goes in v1:
time: 89.8 us; the launch traced here: 89.2 us
  local copies, waits for them, and re-layouts  43.8 us (49%)
  matrix products  13.6 us (15%)
  starting transfers between devices  10.6 us (12%)
  waiting for transfers between devices  9.22 us (10%)
  other arithmetic  6.09 us (7%)
  blocking collectives  5.61 us (6%)
    another operation x2, local copies, waits for them, and re-layouts  12.9 us
    dot_general x2, matrix products, work(): jnp.einsum('abc,bwc->awc', toeplitz_block, sub_piece, preferred_element_t...  11 us
    ppermute x2, waiting for transfers between devices, extended(): lax.ppermute(lax.slice_in_dim(block, 0, width, axis=dim), axis, backward)  9.21 us
    cond x2, local copies, waits for them, and re-layouts  8.31 us
    ppermute x2, starting transfers between devices, extended(): lax.ppermute(lax.slice_in_dim(block, block.shape[dim] - width, None, axis...  5.62 us
    all_to_all x1, blocking collectives, on_device(): lax.all_to_all(jnp.stack([product] * lax.axis_size('row')), 'row', 0, 0)  5.61 us
    another operation x4, local copies, waits for them, and re-layouts, toeplitz(): tiled = jnp.tile(window, (out_count + 1, 1))  4.96 us
    ppermute x2, starting transfers between devices, extended(): lax.ppermute(lax.slice_in_dim(block, 0, width, axis=dim), axis, backward)  4.95 us
  transfers between devices with their start and end apart: 4, of which 1 were waited for; matrix products, arithmetic and copies ran while one was open for 1% of the time, Pallas kernels for 0%

profile of v1, /device:TPU:127, one launch (start us, length us, event | category | flops | bytes accessed | tf_op | source)
XLA Modules:
  0.0 89.2 jit_solution(1491118594156590473)
XLA Ops:
  0.0 1.0 %copy-done = bf16[32,32,256]{2,1,0:T(8,128)(2,1)S(1)} copy-done((bf16[32,32,256]{2,1,0:T(8,128)(2,1)S(1)}, bf16[32,32,256]{2,1,0:T(8,128)(2,1)}, u32[]{:S(2)}) %copy-start) | copy-done | bytes 524312
  1.0 1.6 %convolution_convert_fusion = bf16[1024,768]{1,0:T(8,128)(2,1)S(1)} fusion(bf16[1024,256]{1,0:T(8,128)(2,1)S(1)} %bitcast.26, bf16[256,768]{1,0:T(8,128)(2,1)} %param.12), kind=kOutput, calls=%fused_computation.9 | convolution fusion | flops 403439616 | bytes 2490368 | tf_op jit(solution)/shard_map/dot_general | solution.py:47
  2.6 1.3 %collective-permute-start = (bf16[1,32,768]{2,1,0:T(8,128)(2,1)S(1)}, bf16[1,32,768]{2,1,0:T(8,128)(2,1)S(1)}, u32[]{:S(2)}, u32[]{:S(2)}) collective-permute-start(bf16[1,32,768]{2,1,0:T(8,128)(2,1)S(1)} %get-tuple-element.58), channel_id=1, source_target_pairs={{0,128},{1,129},{2,130},{3,131},{4,132},{5,133},{6,134},{7,135},{8... | collective-permute-start | bytes 147464 | tf_op jit(solution)/shard_map/ppermute | solution.py:12
  3.9 3.0 %collective-permute-start.1 = (bf16[1,32,768]{2,1,0:T(8,128)(2,1)S(1)}, bf16[1,32,768]{2,1,0:T(8,128)(2,1)S(1)}, u32[]{:S(2)}, u32[]{:S(2)}) collective-permute-start(bf16[1,32,768]{2,1,0:T(8,128)(2,1)S(1)} %get-tuple-element.59), channel_id=1, source_target_pairs={{128,0},{129,1},{130,2},{131,3},{132,4},{133,5},{134,6},{135,7},{1... | collective-permute-start | bytes 147464 | tf_op jit(solution)/shard_map/ppermute | solution.py:15
  7.0 0.8 concatenate.31
  8.1 4.3 %collective-permute-start.2 = (bf16[34,1,768]{2,1,0:T(2,128)(2,1)S(1)}, bf16[34,1,768]{2,1,0:T(2,128)(2,1)S(1)}, u32[]{:S(2)}, u32[]{:S(2)}) collective-permute-start(bf16[34,1,768]{2,1,0:T(2,128)(2,1)S(1)} %get-tuple-element.56), channel_id=1, source_target_pairs={{0,1},{1,2},{2,3},{3,4},{4,5},{5,6},{6,7},{7,8},{8,9},{9,10},{10,1... | collective-permute-start | bytes 156680 | tf_op jit(solution)/shard_map/ppermute | solution.py:12
  12.4 1.9 %collective-permute-start.3 = (bf16[34,1,768]{2,1,0:T(2,128)(2,1)S(1)}, bf16[34,1,768]{2,1,0:T(2,128)(2,1)S(1)}, u32[]{:S(2)}, u32[]{:S(2)}) collective-permute-start(bf16[34,1,768]{2,1,0:T(2,128)(2,1)S(1)} %get-tuple-element.57), channel_id=1, source_target_pairs={{1,0},{2,1},{3,2},{4,3},{5,4},{6,5},{7,6},{8,7},{9,8},{10,9},{11,1... | collective-permute-start | bytes 156680 | tf_op jit(solution)/shard_map/ppermute | solution.py:15
  14.5 9.2 %collective-permute-done.3 = bf16[34,1,768]{2,1,0:T(2,128)(2,1)S(1)} collective-permute-done((bf16[34,1,768]{2,1,0:T(2,128)(2,1)S(1)}, bf16[34,1,768]{2,1,0:T(2,128)(2,1)S(1)}, u32[]{:S(2)}, u32[]{:S(2)}) %collective-permute-start.3) | collective-permute-done | bytes 52256 | tf_op jit(solution)/shard_map/ppermute | solution.py:15
  23.7 1.2 %maximum_maximum_fusion = (bf16[34,33,768]{2,1,0:T(8,128)(2,1)S(1)}, bf16[34,33,768]{2,1,0:T(8,128)(2,1)S(1)}) fusion(bf16[1,32,768]{2,1,0:T(8,128)(2,1)S(1)} %collective-permute-done.1, bf16[32,32,768]{2,1,0:T(8,128)(2,1)S(1)} %bitcast.28, bf16[1,32,768]{2,1,0:T(8,128)(2,1)S(1)} %collective-permute-done, bf16[34,1,768]{2,1,0:T(2,128)(2,1)S(1)} %collective-permute-done.2, ...), kind=kLoop, calls=%fused_computation.7 | loop fusion | flops 13787136 | bytes 5222400 | tf_op jit(solution)/shard_map/concatenate | solution.py:16
  24.9 4.1 %add_convert_fusion = bf16[32,32,768]{2,1,0:T(8,128)(2,1)S(1)} fusion(bf16[32,32,768]{2,1,0:T(8,128)(2,1)S(1)} %bitcast.29, bf16[34,33,768]{2,1,0:T(8,128)(2,1)S(1)} %get-tuple-element.55, bf16[1,32,768]{2,1,0:T(8,128)(2,1)S(1)} %collective-permute-done.1, bf16[34,33,768]{2,1,0:T(8,128)(2,1)S(1)} %get-tuple-element.54, ...), kind=kLoop, calls=%fused_computation.6 | loop fusion | flops 23592960 | bytes 12711936 | tf_op jit(solution)/shard_map/convert_element_type | solution.py:28
  29.0 1.2 %copy-done.1 = bf16[32,32,768]{2,1,0:T(8,128)(2,1)} copy-done((bf16[32,32,768]{2,1,0:T(8,128)(2,1)}, bf16[32,32,768]{2,1,0:T(8,128)(2,1)S(1)}, u32[]{:S(2)}) %copy-start.1) | copy-done | bytes 1572888
  30.4 5.6 %all_to_all.5 = bf16[2,32,32,256]{3,2,1,0:T(8,128)(2,1)S(1)} all-to-all(bf16[2,32,32,256]{3,2,1,0:T(8,128)(2,1)S(1)} %pad_maximum_fusion.3), channel_id=1, replica_groups=mesh['row'=2,'col'=128] {'row'}, dimensions={0} | all-to-all | bytes 2097152 | tf_op jit(solution)/shard_map/all_to_all | solution.py:62
  36.1 20.3 %conditional.2 = (f32[32,32,256]{1,0,2:T(8,128)}) conditional(s32[]{:T(128)} %convert_element_type.91, () %tuple.17, (s32[]{:T(128)}, bf16[384,256]{1,0:T(8,128)(2,1)S(1)}, bf16[2,32,32,256]{3,2,1,0:T(8,128)(2,1)S(1)}) %tuple.18), branch_computations={%region_0.1_spmd, %region_1.2_spmd} | conditional | flops 16777220 | bytes 16790586 | solution.py:80
  36.2 1.3 %tile.10 = bf16[2079,256]{1,0:T(8,128)(2,1)} reshape(bf16[33,63,256]{2,1,0:T(8,128)(2,1)S(1)} %tile.4) | data formatting | bytes 2128896 | tf_op jit(solution)/shard_map/cond/branch_1_fun/tile | solution.py:39
  37.5 1.5 %slice.141 = bf16[1984,256]{1,0:T(8,128)(2,1)S(1)} slice(bf16[2079,256]{1,0:T(8,128)(2,1)} %tile.10), slice={[31:2015], [0:256]} | slice | bytes 2031616 | tf_op jit(solution)/shard_map/cond/branch_1_fun/slice | solution.py:40
  39.0 1.3 %reshape.28 = bf16[32,62,256]{2,1,0:T(8,128)(2,1)} reshape(bf16[1984,256]{1,0:T(8,128)(2,1)S(1)} %slice.141) | data formatting | bytes 2031616 | tf_op jit(solution)/shard_map/cond/branch_1_fun/reshape | solution.py:41
  40.2 1.1 %slice.142 = bf16[32,32,256]{2,1,0:T(8,128)(2,1)S(1)} slice(bf16[32,62,256]{2,1,0:T(8,128)(2,1)} %reshape.28), slice={[0:32], [0:32], [0:256]} | slice | bytes 1048576 | tf_op jit(solution)/shard_map/cond/branch_1_fun/slice | solution.py:41
  41.3 3.8 %copy.24 = bf16[32,32,256]{1,0,2:T(8,128)(2,1)} copy(bf16[32,32,256]{2,1,0:T(8,128)(2,1)S(1)} %slice.142) | data formatting | bytes 1048576 | tf_op jit(solution)/shard_map/cond
  45.1 6.4 %copy.19 = bf16[2,32,32,256]{2,1,3,0:T(8,128)(2,1)} copy(bf16[2,32,32,256]{3,2,1,0:T(8,128)(2,1)S(1)} %get-tuple-element.39) | data formatting | bytes 2097152 | tf_op jit(solution)/shard_map
  51.5 4.9 %convolution_bitcast_fusion = f32[32,32,256]{1,0,2:T(8,128)} fusion(bf16[32,32,256]{1,0,2:T(8,128)(2,1)} %copy.24, bf16[2,32,32,256]{2,1,3,0:T(8,128)(2,1)} %copy.19), kind=kOutput, calls=%fused_computation | convolution fusion | flops 16777216 | bytes 5242880 | tf_op jit(solution)/shard_map/cond/branch_1_fun/abc,bwc->awc/dot_general | solution.py:73
  56.4 30.8 %conditional.3 = (f32[32,32,256]{2,1,0:T(8,128)S(1)}) conditional(s32[]{:T(128)} %convert_element_type.90, f32[32,32,256]{1,0,2:T(8,128)} %get-tuple-element.62, (s32[]{:T(128)}, bf16[384,256]{1,0:T(8,128)(2,1)S(1)}, bf16[2,32,32,256]{3,2,1,0:T(8,128)(2,1)S(1)}, f32[32,32,256]{1,0,2:T(8,128)}) %tuple.19), branch_computations={%region_2.3_spmd, %region_3.4_spmd} | conditional | flops 17039364 | bytes 23082054 | solution.py:80
  56.4 1.2 %tile.11 = bf16[33,63,256]{2,1,0:T(8,128)(2,1)} broadcast(bf16[63,256]{1,0:T(8,128)(2,1)S(1)} %constant_dynamic-slice_fusion.1), dimensions={1,2} | broadcast | bytes 1096704 | tf_op jit(solution)/shard_map/cond/branch_1_fun/tile | solution.py:39
  57.6 2.4 %tile.12 = bf16[2079,256]{1,0:T(8,128)(2,1)} reshape(bf16[33,63,256]{2,1,0:T(8,128)(2,1)} %tile.11) | data formatting | bytes 2128896 | tf_op jit(solution)/shard_map/cond/branch_1_fun/tile | solution.py:39
  60.0 2.4 %slice.144 = bf16[1984,256]{1,0:T(8,128)(2,1)} slice(bf16[2079,256]{1,0:T(8,128)(2,1)} %tile.12), slice={[31:2015], [0:256]} | slice | bytes 2031616 | tf_op jit(solution)/shard_map/cond/branch_1_fun/slice | solution.py:40
  62.4 2.3 %reshape.29 = bf16[32,62,256]{2,1,0:T(8,128)(2,1)} reshape(bf16[1984,256]{1,0:T(8,128)(2,1)} %slice.144) | data formatting | bytes 2031616 | tf_op jit(solution)/shard_map/cond/branch_1_fun/reshape | solution.py:41
  64.7 1.9 %slice.145 = bf16[32,32,256]{2,1,0:T(8,128)(2,1)} slice(bf16[32,62,256]{2,1,0:T(8,128)(2,1)} %reshape.29), slice={[0:32], [0:32], [0:256]} | slice | bytes 1048576 | tf_op jit(solution)/shard_map/cond/branch_1_fun/slice | solution.py:41
  66.6 4.6 %copy.25 = bf16[32,32,256]{1,0,2:T(8,128)(2,1)} copy(bf16[32,32,256]{2,1,0:T(8,128)(2,1)} %slice.145) | data formatting | bytes 1048576 | tf_op jit(solution)/shard_map/cond
  71.1 6.4 %copy.20 = bf16[2,32,32,256]{2,1,3,0:T(8,128)(2,1)} copy(bf16[2,32,32,256]{3,2,1,0:T(8,128)(2,1)S(1)} %get-tuple-element.42) | data formatting | bytes 2097152 | tf_op jit(solution)/shard_map
  77.6 6.1 %bitcast_add_fusion = f32[32,32,256]{1,0,2:T(8,128)} fusion(f32[32,32,256]{1,0,2:T(8,128)} %get-tuple-element.31, bf16[32,32,256]{1,0,2:T(8,128)(2,1)} %copy.25, bf16[2,32,32,256]{2,1,3,0:T(8,128)(2,1)} %copy.20), kind=kOutput, calls=%fused_computation.3 | convolution fusion | flops 17039360 | bytes 9437184 | tf_op jit(solution)/shard_map/cond/branch_1_fun/abc,bwc->awc/dot_general | solution.py:73
  83.7 3.5 %copy.23 = f32[32,32,256]{2,1,0:T(8,128)S(1)} copy(f32[32,32,256]{1,0,2:T(8,128)} %bitcast_add_fusion) | data formatting | bytes 2097152 | tf_op jit(solution)/shard_map/cond | solution.py:80
  87.5 0.6 copy-done.3
  88.1 1.1 %convolution_convert_fusion.1 = bf16[1024,256]{1,0:T(8,128)(2,1)} fusion(bf16[1024,256]{1,0:T(8,128)(2,1)S(1)} %bitcast.30, bf16[256,256]{1,0:T(8,128)(2,1)S(1)} %copy-done.3), kind=kOutput, calls=%fused_computation.12 | convolution fusion | flops 134479872 | bytes 1179648 | tf_op jit(solution)/shard_map/dot_general | solution.py:83
  (26 shorter events, 1.1 us)
Async XLA Ops:
  0.0 1.0 %copy-start = (bf16[32,32,256]{2,1,0:T(8,128)(2,1)S(1)}, bf16[32,32,256]{2,1,0:T(8,128)(2,1)}, u32[]{:S(2)}) copy-start(bf16[32,32,256]{2,1,0:T(8,128)(2,1)} %param.11) | copy-start | bytes 1572868
  0.0 14.3 %copy-start.4 = (bf16[3,3,768]{2,1,0:T(4,128)(2,1)S(1)}, bf16[3,3,768]{2,1,0:T(4,128)(2,1)}, u32[]{:S(2)}) copy-start(bf16[3,3,768]{2,1,0:T(4,128)(2,1)} %param.13) | copy-start | bytes 41476
  2.6 5.3 %collective-permute-start = (bf16[1,32,768]{2,1,0:T(8,128)(2,1)S(1)}, bf16[1,32,768]{2,1,0:T(8,128)(2,1)S(1)}, u32[]{:S(2)}, u32[]{:S(2)}) collective-permute-start(bf16[1,32,768]{2,1,0:T(8,128)(2,1)S(1)} %get-tuple-element.58), channel_id=1, source_target_pairs={{0,128},{1,129},{2,130},{3,131},{4,132},{5,133},{6,134},{7,135},{8... | collective-permute-start | bytes 147464 | tf_op jit(solution)/shard_map/ppermute | solution.py:12
  3.9 4.0 %collective-permute-start.1 = (bf16[1,32,768]{2,1,0:T(8,128)(2,1)S(1)}, bf16[1,32,768]{2,1,0:T(8,128)(2,1)S(1)}, u32[]{:S(2)}, u32[]{:S(2)}) collective-permute-start(bf16[1,32,768]{2,1,0:T(8,128)(2,1)S(1)} %get-tuple-element.59), channel_id=1, source_target_pairs={{128,0},{129,1},{130,2},{131,3},{132,4},{133,5},{134,6},{135,7},{1... | collective-permute-start | bytes 147464 | tf_op jit(solution)/shard_map/ppermute | solution.py:15
  8.1 16.8 %copy-start.5 = (f32[768]{0:T(1024)S(1)}, f32[768]{0:T(1024)}, u32[]{:S(2)}) copy-start(f32[768]{0:T(1024)} %param.14) | copy-start | bytes 9220
  8.1 6.4 %collective-permute-start.2 = (bf16[34,1,768]{2,1,0:T(2,128)(2,1)S(1)}, bf16[34,1,768]{2,1,0:T(2,128)(2,1)S(1)}, u32[]{:S(2)}, u32[]{:S(2)}) collective-permute-start(bf16[34,1,768]{2,1,0:T(2,128)(2,1)S(1)} %get-tuple-element.56), channel_id=1, source_target_pairs={{0,1},{1,2},{2,3},{3,4},{4,5},{5,6},{6,7},{7,8},{8,9},{9,10},{10,1... | collective-permute-start | bytes 156680 | tf_op jit(solution)/shard_map/ppermute | solution.py:12
  12.4 11.3 %collective-permute-start.3 = (bf16[34,1,768]{2,1,0:T(2,128)(2,1)S(1)}, bf16[34,1,768]{2,1,0:T(2,128)(2,1)S(1)}, u32[]{:S(2)}, u32[]{:S(2)}) collective-permute-start(bf16[34,1,768]{2,1,0:T(2,128)(2,1)S(1)} %get-tuple-element.57), channel_id=1, source_target_pairs={{1,0},{2,1},{3,2},{4,3},{5,4},{6,5},{7,6},{8,7},{9,8},{10,9},{11,1... | collective-permute-start | bytes 156680 | tf_op jit(solution)/shard_map/ppermute | solution.py:15
  29.0 1.2 %copy-start.1 = (bf16[32,32,768]{2,1,0:T(8,128)(2,1)}, bf16[32,32,768]{2,1,0:T(8,128)(2,1)S(1)}, u32[]{:S(2)}) copy-start(bf16[32,32,768]{2,1,0:T(8,128)(2,1)S(1)} %add_convert_fusion) | copy-start | bytes 4718596
  56.4 30.8 %copy-start.2 = (bf16[32,32,768]{2,1,0:T(8,128)(2,1)S(1)}, bf16[32,32,768]{2,1,0:T(8,128)(2,1)}, u32[]{:S(2)}) copy-start(bf16[32,32,768]{2,1,0:T(8,128)(2,1)} %copy-done.1) | copy-start | bytes 4718596
  56.4 30.8 %copy-start.6 = (f32[256]{0:T(256)S(1)}, f32[256]{0:T(256)}, u32[]{:S(2)}) copy-start(f32[256]{0:T(256)} %param.16) | copy-start | bytes 3076
  87.2 0.9 %copy-start.3 = (bf16[256,256]{1,0:T(8,128)(2,1)S(1)}, bf16[256,256]{1,0:T(8,128)(2,1)}, u32[]{:S(2)}) copy-start(bf16[256,256]{1,0:T(8,128)(2,1)} %param.17) | copy-start | bytes 393220
